TPU v7x, 256 devices: a whole 4x4x8 slice. The times are simulated.
256 devices in a mesh: seq: 64 (over x, z, core), head: 4 (over y).
Axes of the slice: x: 4, y: 4, z: 8, core: 2. Of those that a mesh axis runs over, the one named last changes fastest.
Arguments:
- queries: bfloat16 [32768, 4096], P('seq', 'head'), may hold values from -6 to 6
- key_input: bfloat16 [32768, 4096], P('seq', 'head'), may hold values from -6 to 6
- value_input: bfloat16 [32768, 4096], P('seq', 'head'), may hold values from -40 to 40
- gate_input: bfloat16 [32768, 4096], P('seq', 'head'), may hold values from -8 to 8
- kv_state: float32 [32, 128, 128], P('head'), may hold values from -512 to 512
- norm_gain: float32 [4096], replicated, may hold values from 0.25 to 1.75
- out_weight: bfloat16 [4096, 4096], P('head', 'seq'), may hold values from -0.09375 to 0.09375
Outputs:
- output: bfloat16 [32768, 4096], P(('seq', 'head'))
All inputs are finite; a program needn't handle non-finite values.
Results may differ from a plain program's by a relative error of at most 0.02.
Values may be sent and summed in bfloat16 or wider, within the bound.
A program may use at most 128 MiB of HBM per device.

v0:
```python
import jax
import jax.numpy as jnp
from jax import lax
from jax.sharding import PartitionSpec as P

DH = 128
BLOCK = 512
epsilon = 1e-05


def entering(value, axis, join, neutral):
    place = lax.axis_index(axis)
    gathered = lax.all_gather(value.astype(jnp.bfloat16), axis)
    state = jnp.zeros_like(value) + jnp.asarray(neutral, value.dtype)

    def one(turn, state):
        return join(state, lax.dynamic_index_in_dim(gathered, turn, 0, False).astype(value.dtype))

    return lax.fori_loop(0, place, one, state)


def add_states(earlier, later):
    return earlier + later


def gated_norm(attn_rows, gate_rows, gain_part, total_width, square_sum):
    attn_float = attn_rows.astype(jnp.float32)
    scale = lax.rsqrt(square_sum / total_width + epsilon)
    normed = attn_float * scale[:, None] * gain_part[None, :]
    return (normed * jax.nn.sigmoid(gate_rows.astype(jnp.float32))).astype(jnp.bfloat16)


def shards(queries, key_input, value_input, gate_input, kv_state, norm_gain, out_weight):
    tok_rows = queries.shape[0]
    local_width = queries.shape[1]
    local_heads = local_width // DH
    num_blocks = tok_rows // BLOCK
    block_shape = (num_blocks, BLOCK, local_heads, DH)
    q_blocks = queries.reshape(block_shape)
    k_blocks = key_input.reshape(block_shape)
    v_blocks = value_input.reshape(block_shape)
    block_states = jnp.einsum(
        "nthd,nthe->nhde", k_blocks, v_blocks, preferred_element_type=jnp.float32
    )
    own_total = jnp.sum(block_states, axis=0)
    prefix = entering(own_total, "seq", add_states, jnp.zeros_like(own_total))
    start_state = kv_state + prefix
    running = jnp.cumsum(block_states, axis=0) - block_states
    before = start_state[None] + running
    carried_part = jnp.einsum(
        "nthd,nhde->nthe", q_blocks.astype(jnp.float32), before, precision=lax.Precision.HIGHEST
    )
    scores = jnp.einsum("nthd,nshd->nhts", q_blocks, k_blocks, preferred_element_type=jnp.float32)
    causal = jnp.arange(BLOCK)[:, None] >= jnp.arange(BLOCK)[None, :]
    weights = jnp.where(causal[None, None], scores, 0.0).astype(jnp.bfloat16)
    inner_part = jnp.einsum(
        "nhts,nshe->nthe", weights, v_blocks, preferred_element_type=jnp.float32
    )
    attn = (carried_part + inner_part).astype(jnp.bfloat16).reshape(tok_rows, local_width)
    total_width = local_width * lax.axis_size("head")
    tok_attn, tok_gate = (
        lax.all_to_all(attn, "head", split_axis=0, concat_axis=1, tiled=True),
        lax.all_to_all(gate_input, "head", split_axis=0, concat_axis=1, tiled=True),
    )
    tok_float = tok_attn.astype(jnp.float32)
    normed = gated_norm(
        tok_attn, tok_gate, norm_gain, total_width, jnp.sum(tok_float * tok_float, axis=1)
    )
    hidden = lax.all_to_all(normed, "head", split_axis=1, concat_axis=0, tiled=True)
    terms = jnp.dot(
        hidden,
        lax.all_gather(out_weight, "seq", axis=1, tiled=True),
        preferred_element_type=jnp.float32,
    )
    return lax.psum_scatter(terms.astype(jnp.bfloat16), "head", scatter_dimension=0, tiled=True)


def solution(mesh):
    in_specs = (
        P("seq", "head"),
        P("seq", "head"),
        P("seq", "head"),
        P("seq", "head"),
        P("head", None, None),
        P(),
        P("head", "seq"),
    )
    out_specs = P(("seq", "head"), None)
    return jax.shard_map(shards, mesh=mesh, in_specs=in_specs, out_specs=out_specs, check_vma=False)
```

profile of v0, /device:TPU:1, one launch (start us, length us, event | category | flops | bytes accessed | tf_op | source)
XLA Modules:
  0.0 307.6 jit_solution(3969963221888918470)
XLA Ops:
  6.5 0.0 copy-start
  6.5 0.0 all-gather.6.cloned.1.call-start
  6.5 2.9 fusion.34
  9.4 0.0 all-gather.6.cloned.1.call-update
  9.4 0.0 all-gather.4.cloned.1.call-start
  9.5 0.7 all-gather.4.cloned.1.call-update
  10.2 0.1 iota_compare_fusion
  10.3 103.8 %all-gather.6.cloned.1.call-done = bf16[512,128,128]{2,1,0:T(8,128)(2,1)} async-done(((bf16[8,128,128]{2,1,0:T(8,128)(2,1)}), bf16[512,128,128]{2,1,0:T(8,128)(2,1)}) %all-gather.6.cloned.1.call-update) | async-done | bytes 16777232 | tf_op jit(solution)/shard_map/all_gather | solution.py:13
  114.1 0.0 copy-start.2
  114.1 1.2 while.10
  114.1 1.1 convert_add_fusion.2
  115.3 0.0 copy-done
  115.3 0.0 copy-done.2
  115.3 2.4 fusion.13
  117.7 4.8 %fusion.10 = bf16[1,512,8,128]{1,3,2,0:T(8,128)(2,1)S(1)} fusion(f32[8,128,512]{2,1,0:T(8,128)} %fusion.13, pred[512,512]{1,0:T(8,128)(4,1)S(1)} %iota_compare_fusion, bf16[512,1024]{1,0:T(8,128)(2,1)S(1)} %copy-done, bf16[512,1024]{1,0:T(8,128)(2,1)} %param.11, bf16[512,1024]{1,0:T(8,128)(2,1)} %param.10), kind=kOutput, calls=%fused_computation.15 | convolution fusion | flops 1078984704 | bytes 6553600 | tf_op jit(solution)/shard_map/nhts,nshe->nthe/dot_general | solution.py:56
  122.5 0.3 all_to_all.32
  122.8 0.0 copy-start.1
  122.8 1.1 copy.40
  123.9 4.0 %all-to-all-start = ((bf16[4,128,1024]{1,2,0:T(8,128)(2,1)}), bf16[4,128,1024]{1,2,0:T(8,128)(2,1)S(1)}, u32[]{:S(2)}, u32[]{:S(2)}) async-start(bf16[4,128,1024]{1,2,0:T(8,128)(2,1)} %copy.40), calls=%async_computation | async-start | bytes 2097152 | tf_op jit(solution)/shard_map/all_to_all | solution.py:62
  127.9 0.0 copy-done.1
  127.9 0.0 copy-start.3
  128.0 1.3 copy.41
  129.3 13.6 %all-to-all-done = bf16[4,128,1024]{1,2,0:T(8,128)(2,1)S(1)} async-done(((bf16[4,128,1024]{1,2,0:T(8,128)(2,1)}), bf16[4,128,1024]{1,2,0:T(8,128)(2,1)S(1)}, u32[]{:S(2)}, u32[]{:S(2)}) %all-to-all-start) | async-done | bytes 1048608 | tf_op jit(solution)/shard_map/all_to_all | solution.py:62
  142.8 3.5 %all-to-all-start.1 = ((bf16[4,128,1024]{1,2,0:T(8,128)(2,1)}), bf16[4,128,1024]{1,2,0:T(8,128)(2,1)S(1)}, u32[]{:S(2)}, u32[]{:S(2)}) async-start(bf16[4,128,1024]{1,2,0:T(8,128)(2,1)} %copy.41), calls=%async_computation.1 | async-start | bytes 2097152 | tf_op jit(solution)/shard_map/all_to_all | solution.py:63
  146.3 0.0 reduce-scatter.2.cloned.1.call-start
  146.4 0.0 copy-done.3
  146.4 0.6 fusion.5
  147.0 13.3 %all-to-all-done.1 = bf16[4,128,1024]{1,2,0:T(8,128)(2,1)S(1)} async-done(((bf16[4,128,1024]{1,2,0:T(8,128)(2,1)}), bf16[4,128,1024]{1,2,0:T(8,128)(2,1)S(1)}, u32[]{:S(2)}, u32[]{:S(2)}) %all-to-all-start.1) | async-done | bytes 1048608 | tf_op jit(solution)/shard_map/all_to_all | solution.py:63
  160.2 0.8 fusion.21
  161.0 15.2 %all_to_all.42 = bf16[128,4,1024]{0,2,1:T(8,128)(2,1)S(1)} all-to-all(bf16[128,4,1024]{0,2,1:T(8,128)(2,1)S(1)} %fusion.21), channel_id=1, replica_groups=mesh['seq'=64,'head'=4] {'head'}, dimensions={1} | all-to-all | bytes 2097152 | tf_op jit(solution)/shard_map/all_to_all | solution.py:69
  176.2 0.5 copy.42
  176.7 20.2 %all-gather.4.cloned.1.call-done = bf16[1024,4096]{0,1:T(8,128)(2,1)} async-done(((bf16[1024,64]{0,1:T(8,128)(2,1)}), bf16[1024,4096]{0,1:T(8,128)(2,1)}) %all-gather.4.cloned.1.call-update) | async-done | bytes 8388624 | tf_op jit(solution)/shard_map/all_gather | solution.py:72
  196.9 9.4 %convolution_convert_fusion = bf16[512,4096]{1,0:T(8,128)(2,1)} fusion(bf16[512,1024]{1,0:T(8,128)(2,1)S(1)} %bitcast.73, bf16[1024,4096]{0,1:T(8,128)(2,1)} %all-gather.4.cloned.1.call-done), kind=kOutput, calls=%fused_computation.2 | convolution fusion | flops 4297064448 | bytes 13631488 | tf_op jit(solution)/shard_map/dot_general | solution.py:70
  206.3 0.0 reduce-scatter.2.cloned.1.call-update
  206.4 94.8 %reduce-scatter.2.cloned.1.call-done = bf16[128,4096]{1,0:T(8,128)(2,1)} async-done(((bf16[512,4096]{1,0:T(8,128)(2,1)}), bf16[128,4096]{1,0:T(8,128)(2,1)}) %reduce-scatter.2.cloned.1.call-update) | async-done | bytes 1048592 | tf_op jit(solution)/shard_map/reduce_scatter | solution.py:75
  (3 shorter events, 0.1 us)
Async XLA Ops:
  6.5 108.7 %copy-start = (bf16[512,1024]{1,0:T(8,128)(2,1)S(1)}, bf16[512,1024]{1,0:T(8,128)(2,1)}, u32[]{:S(2)}) copy-start(bf16[512,1024]{1,0:T(8,128)(2,1)} %param.9) | copy-start | bytes 3145732
  6.5 107.5 %all-gather.6.cloned.1.call-start = ((), (), s32[]{:S(2)}) async-start(), calls=%async_computation.6 | async-start | bytes 17039360 | tf_op jit(solution)/shard_map/all_gather | solution.py:13
  9.4 187.4 %all-gather.4.cloned.1.call-start = ((), (), s32[]{:S(2)}) async-start(), calls=%async_computation.4 | async-start | bytes 8519680 | tf_op jit(solution)/shard_map/all_gather | solution.py:72
  114.1 1.2 copy-start.2
  122.8 5.1 %copy-start.1 = (bf16[512,1024]{1,0:T(8,128)(2,1)S(1)}, bf16[512,1024]{1,0:T(8,128)(2,1)}, u32[]{:S(2)}) copy-start(bf16[512,1024]{1,0:T(8,128)(2,1)} %param.12) | copy-start | bytes 3145732
  123.9 18.9 %all-to-all-start = ((bf16[4,128,1024]{1,2,0:T(8,128)(2,1)}), bf16[4,128,1024]{1,2,0:T(8,128)(2,1)S(1)}, u32[]{:S(2)}, u32[]{:S(2)}) async-start(bf16[4,128,1024]{1,2,0:T(8,128)(2,1)} %copy.40), calls=%async_computation | async-start | bytes 2097152 | tf_op jit(solution)/shard_map/all_to_all | solution.py:62
  127.9 18.4 %copy-start.3 = (f32[4096]{0:T(1024)S(1)}, f32[4096]{0:T(1024)}, u32[]{:S(2)}) copy-start(f32[4096]{0:T(1024)} %param.14) | copy-start | bytes 49156
  142.8 17.4 %all-to-all-start.1 = ((bf16[4,128,1024]{1,2,0:T(8,128)(2,1)}), bf16[4,128,1024]{1,2,0:T(8,128)(2,1)S(1)}, u32[]{:S(2)}, u32[]{:S(2)}) async-start(bf16[4,128,1024]{1,2,0:T(8,128)(2,1)} %copy.41), calls=%async_computation.1 | async-start | bytes 2097152 | tf_op jit(solution)/shard_map/all_to_all | solution.py:63
  146.3 154.8 %reduce-scatter.2.cloned.1.call-start = ((), (), s32[]{:S(2)}) async-start(), calls=%async_computation.5 | async-start | bytes 5242880 | tf_op jit(solution)/shard_map/reduce_scatter | solution.py:75
Sparse Core Ops, SparseCore 0:
  10.1 103.8 all-gather.5
  116.8 79.9 all-gather.3
  206.5 94.5 reduce-scatter.1
where the time goes:
time: 310 us; the launch traced here: 308 us
  waiting for transfers between devices  246 us (79%)
  matrix products  19.5 us (6%)
  blocking collectives  15.2 us (5%)
  between operations  13.2 us (4%)
  starting transfers between devices  7.63 us (2%)
  local copies, waits for them, and re-layouts  3.29 us (1%)
    all_gather x1, waiting for transfers between devices, entering(): gathered = lax.all_gather(value.astype(jnp.bfloat16), axis)  104 us
    reduce_scatter x1, waiting for transfers between devices, shards(): lax.psum_scatter(terms.astype(jnp.bfloat16), 'head', scatter_dimension=0,...  94.8 us
    all_gather x1, waiting for transfers between devices, shards(): lax.all_gather(out_weight, 'seq', axis=1, tiled=True)  20.2 us
    all_to_all x1, blocking collectives, shards(): lax.all_to_all(normed, 'head', split_axis=1, concat_axis=0, tiled=True)  15.2 us
    all_to_all x1, waiting for transfers between devices, shards(): lax.all_to_all(attn, 'head', split_axis=0, concat_axis=1, tiled=True)  13.6 us
    all_to_all x1, waiting for transfers between devices, shards(): lax.all_to_all(gate_input, 'head', split_axis=0, concat_axis=1, tiled=True)  13.3 us
    dot_general x1, matrix products, shards(): jnp.dot(hidden, lax.all_gather(out_weight, 'seq', axis=1, tiled=True), pr...  9.44 us
  transfers between devices with their start and end apart: 5, of which 5 were waited for; matrix products, arithmetic and copies ran while one was open for 4% of the time, Pallas kernels for 0%

commit v1 on v0

--- a/solution.py
+++ b/solution.py
@@ -2,6 +2,7 @@
 import jax.numpy as jnp
 from jax import lax
 from jax.sharding import PartitionSpec as P
+from jax.lax import all_to_all, axis_size
 
 DH = 128
 BLOCK = 512
@@ -31,6 +32,14 @@
 
 
 def shards(queries, key_input, value_input, gate_input, kv_state, norm_gain, out_weight):
+
+    def bind_the_frame(vec):
+        vec_out = jnp.concatenate(
+            all_to_all(jnp.stack(jnp.split(vec, axis_size("head"), axis=1), axis=0), "head", 0, 0),
+            axis=0,
+        )
+        return vec_out
+
     tok_rows = queries.shape[0]
     local_width = queries.shape[1]
     local_heads = local_width // DH
@@ -66,7 +75,7 @@
     normed = gated_norm(
         tok_attn, tok_gate, norm_gain, total_width, jnp.sum(tok_float * tok_float, axis=1)
     )
-    hidden = lax.all_to_all(normed, "head", split_axis=1, concat_axis=0, tiled=True)
+    hidden = bind_the_frame(normed)
     terms = jnp.dot(
         hidden,
         lax.all_gather(out_weight, "seq", axis=1, tiled=True),

time: 310 us -> 297 us (0.958)
  waiting for transfers between devices: 246 us -> 222 us
  other arithmetic: 2.52 us -> 5.67 us
    all_to_all x1, waiting for transfers between devices: 13.3 us -> 0.01 us  [shards(): lax.all_to_all(gate_input, 'head', split_axis=0, concat_axis=1, tiled=True)]
    reduce_scatter x1, waiting for transfers between devices: 94.8 us -> 81.5 us  [shards(): lax.psum_scatter(terms.astype(jnp.bfloat16), 'head', scatter_dimension=0,...]
    all_gather x1, waiting for transfers between devices: 20.2 us -> 30 us  [shards(): lax.all_gather(out_weight, 'seq', axis=1, tiled=True)]
    all_gather x1, waiting for transfers between devices: 104 us -> 98.8 us  [entering(): gathered = lax.all_gather(value.astype(jnp.bfloat16), axis)]
  transfers between devices with their start and end apart: 5 -> 5, of which waited for: 5 -> 4; matrix products, arithmetic and copies ran while one was open for 4% -> 7% of each run, Pallas kernels for 0% -> 0%
where the time goes in v1:
time: 297 us; the launch traced here: 294 us
  waiting for transfers between devices  222 us (75%)
  matrix products  21.5 us (7%)
  blocking collectives  17.2 us (6%)
  between operations  13.2 us (4%)
  starting transfers between devices  9.06 us (3%)
  local copies, waits for them, and re-layouts  6.02 us (2%)
  other arithmetic  5.67 us (2%)
    all_gather x1, waiting for transfers between devices, entering(): gathered = lax.all_gather(value.astype(jnp.bfloat16), axis)  98.8 us
    reduce_scatter x1, waiting for transfers between devices, shards(): lax.psum_scatter(terms.astype(jnp.bfloat16), 'head', scatter_dimension=0,...  81.5 us
    all_gather x1, waiting for transfers between devices, shards(): lax.all_gather(out_weight, 'seq', axis=1, tiled=True)  30 us
    all_to_all x1, blocking collectives, bind_the_frame(): all_to_all(jnp.stack(jnp.split(vec, axis_size('head'), axis=1), axis=0),...  17.2 us
    all_to_all x1, waiting for transfers between devices, shards(): lax.all_to_all(attn, 'head', split_axis=0, concat_axis=1, tiled=True)  10.6 us
    dot_general x1, matrix products, shards(): jnp.dot(hidden, lax.all_gather(out_weight, 'seq', axis=1, tiled=True), pr...  9.45 us
  transfers between devices with their start and end apart: 5, of which 4 were waited for; matrix products, arithmetic and copies ran while one was open for 7% of the time, Pallas kernels for 0%

profile of v1, /device:TPU:1, one launch (start us, length us, event | category | flops | bytes accessed | tf_op | source)
XLA Modules:
  0.0 294.4 jit_solution(1102798989970370436)
XLA Ops:
  6.5 0.0 copy-start
  6.5 0.0 all-gather.6.cloned.1.call-start
  6.5 2.9 fusion.32
  9.4 0.0 all-gather.6.cloned.1.call-update
  9.4 0.0 all-gather.4.cloned.1.call-start
  9.5 0.7 all-gather.4.cloned.1.call-update
  10.2 5.0 %all-to-all-start.1 = ((bf16[4,128,1024]{2,1,0:T(8,128)(2,1)}), bf16[4,128,1024]{2,1,0:T(8,128)(2,1)S(1)}, u32[]{:S(2)}, u32[]{:S(2)}) async-start(bf16[4,128,1024]{2,1,0:T(8,128)(2,1)} %bitcast.90), calls=%async_computation.1 | async-start | bytes 2097152 | tf_op jit(solution)/shard_map/all_to_all | solution.py:72
  15.2 0.1 iota_compare_fusion
  15.3 98.8 %all-gather.6.cloned.1.call-done = bf16[512,128,128]{2,1,0:T(8,128)(2,1)} async-done(((bf16[8,128,128]{2,1,0:T(8,128)(2,1)}), bf16[512,128,128]{2,1,0:T(8,128)(2,1)}) %all-gather.6.cloned.1.call-update) | async-done | bytes 16777232 | tf_op jit(solution)/shard_map/all_gather | solution.py:14
  114.1 1.1 while.10
  114.1 1.1 convert_add_fusion.2
  115.2 0.0 copy-done
  115.2 3.4 %fusion.12 = f32[8,128,512]{2,1,0:T(8,128)} fusion(f32[8,128,128]{2,1,0:T(8,128)S(1)} %get-tuple-element.42, f32[8,128,128]{2,1,0:T(8,128)} %param.13, f32[8,128,128]{2,1,0:T(8,128)S(1)} %get-tuple-element.28, bf16[512,1024]{1,0:T(8,128)(2,1)S(1)} %copy-done), kind=kOutput, calls=%fused_computation.17 | convolution fusion | flops 805699584 | bytes 4718592 | tf_op jit(solution)/shard_map/nthd,nhde->nthe/dot_general | solution.py:59
  118.6 5.8 %fusion.9 = bf16[1,512,8,128]{1,3,2,0:T(8,128)(2,1)} fusion(f32[8,128,512]{2,1,0:T(8,128)} %fusion.12, pred[512,512]{1,0:T(8,128)(4,1)S(1)} %iota_compare_fusion, bf16[512,1024]{1,0:T(8,128)(2,1)S(1)} %copy-done, bf16[512,1024]{1,0:T(8,128)(2,1)} %param.11, bf16[512,1024]{1,0:T(8,128)(2,1)} %param.10), kind=kOutput, calls=%fused_computation.15 | convolution fusion | flops 1078984704 | bytes 6553600 | tf_op jit(solution)/shard_map/nhts,nshe->nthe/dot_general | solution.py:65
  124.4 1.4 all_to_all.23
  125.8 1.1 copy.40
  126.9 0.0 all-to-all-done.1
  126.9 4.0 %all-to-all-start = ((bf16[4,128,1024]{1,2,0:T(8,128)(2,1)}), bf16[4,128,1024]{1,2,0:T(8,128)(2,1)S(1)}, u32[]{:S(2)}, u32[]{:S(2)}) async-start(bf16[4,128,1024]{1,2,0:T(8,128)(2,1)} %copy.40), calls=%async_computation | async-start | bytes 2097152 | tf_op jit(solution)/shard_map/all_to_all | solution.py:71
  130.9 0.0 reduce-scatter.2.cloned.1.call-start
  130.9 1.9 divide_bitcast_fusion
  132.8 0.0 copy-start.1
  132.8 2.9 copy.41
  135.7 10.6 %all-to-all-done = bf16[4,128,1024]{1,2,0:T(8,128)(2,1)S(1)} async-done(((bf16[4,128,1024]{1,2,0:T(8,128)(2,1)}), bf16[4,128,1024]{1,2,0:T(8,128)(2,1)S(1)}, u32[]{:S(2)}, u32[]{:S(2)}) %all-to-all-start) | async-done | bytes 1048608 | tf_op jit(solution)/shard_map/all_to_all | solution.py:71
  146.3 0.6 multiply_reduce_fusion
  146.9 0.0 copy-done.1
  146.9 1.9 fusion.7
  148.9 0.1 slice_bitcast_fusion.3
  148.9 0.1 pad_maximum_fusion
  149.1 17.2 %all_to_all.31 = bf16[4,128,1024]{1,2,0:T(8,128)(2,1)S(1)} all-to-all(bf16[4,128,1024]{1,2,0:T(8,128)(2,1)S(1)} %pad_maximum_fusion), channel_id=1, replica_groups=mesh['seq'=64,'head'=4] {'head'}, dimensions={0} | all-to-all | bytes 2097152 | tf_op jit(solution)/shard_map/all_to_all | solution.py:38
  166.3 0.5 copy.42
  166.9 30.0 %all-gather.4.cloned.1.call-done = bf16[1024,4096]{0,1:T(8,128)(2,1)} async-done(((bf16[1024,64]{0,1:T(8,128)(2,1)}), bf16[1024,4096]{0,1:T(8,128)(2,1)}) %all-gather.4.cloned.1.call-update) | async-done | bytes 8388624 | tf_op jit(solution)/shard_map/all_gather | solution.py:81
  196.9 9.4 %convolution_convert_fusion = bf16[512,4096]{1,0:T(8,128)(2,1)} fusion(bf16[512,1024]{1,0:T(8,128)(2,1)S(1)} %bitcast.91, bf16[1024,4096]{0,1:T(8,128)(2,1)} %all-gather.4.cloned.1.call-done), kind=kOutput, calls=%fused_computation.2 | convolution fusion | flops 4297064448 | bytes 13631488 | tf_op jit(solution)/shard_map/dot_general | solution.py:79
  206.3 0.0 reduce-scatter.2.cloned.1.call-update
  206.4 81.5 %reduce-scatter.2.cloned.1.call-done = bf16[128,4096]{1,0:T(8,128)(2,1)} async-done(((bf16[512,4096]{1,0:T(8,128)(2,1)}), bf16[128,4096]{1,0:T(8,128)(2,1)}) %reduce-scatter.2.cloned.1.call-update) | async-done | bytes 1048592 | tf_op jit(solution)/shard_map/reduce_scatter | solution.py:84
  (2 shorter events, 0.0 us)
Async XLA Ops:
  6.5 108.7 %copy-start = (bf16[512,1024]{1,0:T(8,128)(2,1)S(1)}, bf16[512,1024]{1,0:T(8,128)(2,1)}, u32[]{:S(2)}) copy-start(bf16[512,1024]{1,0:T(8,128)(2,1)} %param.9) | copy-start | bytes 3145732
  6.5 107.5 %all-gather.6.cloned.1.call-start = ((), (), s32[]{:S(2)}) async-start(), calls=%async_computation.6 | async-start | bytes 17039360 | tf_op jit(solution)/shard_map/all_gather | solution.py:14
  9.4 187.4 %all-gather.4.cloned.1.call-start = ((), (), s32[]{:S(2)}) async-start(), calls=%async_computation.4 | async-start | bytes 8519680 | tf_op jit(solution)/shard_map/all_gather | solution.py:81
  10.2 116.7 %all-to-all-start.1 = ((bf16[4,128,1024]{2,1,0:T(8,128)(2,1)}), bf16[4,128,1024]{2,1,0:T(8,128)(2,1)S(1)}, u32[]{:S(2)}, u32[]{:S(2)}) async-start(bf16[4,128,1024]{2,1,0:T(8,128)(2,1)} %bitcast.90), calls=%async_computation.1 | async-start | bytes 2097152 | tf_op jit(solution)/shard_map/all_to_all | solution.py:72
  126.9 19.4 %all-to-all-start = ((bf16[4,128,1024]{1,2,0:T(8,128)(2,1)}), bf16[4,128,1024]{1,2,0:T(8,128)(2,1)S(1)}, u32[]{:S(2)}, u32[]{:S(2)}) async-start(bf16[4,128,1024]{1,2,0:T(8,128)(2,1)} %copy.40), calls=%async_computation | async-start | bytes 2097152 | tf_op jit(solution)/shard_map/all_to_all | solution.py:71
  130.9 157.0 %reduce-scatter.2.cloned.1.call-start = ((), (), s32[]{:S(2)}) async-start(), calls=%async_computation.5 | async-start | bytes 5242880 | tf_op jit(solution)/shard_map/reduce_scatter | solution.py:84
  132.8 14.1 %copy-start.1 = (f32[4096]{0:T(1024)S(1)}, f32[4096]{0:T(1024)}, u32[]{:S(2)}) copy-start(f32[4096]{0:T(1024)} %param.14) | copy-start | bytes 49156
Sparse Core Ops, SparseCore 0:
  10.1 103.8 all-gather.5
  116.8 80.0 all-gather.3
  206.5 81.3 reduce-scatter.1
